TPU v7x, 32 devices: a whole 2x2x4 slice. The times are simulated.
32 devices in a mesh: row: 16 (over z, y, core), col: 2 (over x).
Axes of the slice: x: 2, y: 2, z: 4, core: 2. Of those that a mesh axis runs over, the one named last changes fastest.
Arguments:
- hidden: bfloat16 [2048, 1152], P('col', 'row'), may hold values from -6 to 6
- caption: bfloat16 [1920, 1152], P('col', 'row'), may hold values from -6 to 6
- lengths: int32 [16], replicated, may hold values from 1 to 120, as said below
- timesteps: int32 [16], replicated, may hold values from 0 to 999
- time_table: float32 [6, 1152, 1000], P(None, 'row'), may hold values from -2 to 2
- shift_table: float32 [6, 1152], P(None, 'row'), may hold values from -2 to 2
- query_weight: bfloat16 [1152, 1152], P('row', 'col'), may hold values from -0.1875 to 0.1875
- query_offset: float32 [1152], P('col'), may hold values from -3 to 3
- key_weight: bfloat16 [1152, 1152], P('row', 'col'), may hold values from -0.1875 to 0.1875
- value_weight: bfloat16 [1152, 1152], P('row', 'col'), may hold values from -0.1875 to 0.1875
- value_offset: float32 [1152], P('col'), may hold values from -3 to 3
- output_weight: bfloat16 [1152, 1152], P('col', 'row'), may hold values from -1 to 1
- output_offset: float32 [1152], P('row'), may hold values from -3 to 3
- probe_weight: bfloat16 [1152, 1152], P('row', 'col'), may hold values from -0.1875 to 0.1875
- probe_offset: float32 [1152], P('col'), may hold values from -3 to 3
- lookup_weight: bfloat16 [1152, 1152], P('row', 'col'), may hold values from -0.1875 to 0.1875
- content_weight: bfloat16 [1152, 1152], P('row', 'col'), may hold values from -0.1875 to 0.1875
- content_offset: float32 [1152], P('col'), may hold values from -3 to 3
- merge_weight: bfloat16 [1152, 1152], P('col', 'row'), may hold values from -1 to 1
- merge_offset: float32 [1152], P('row'), may hold values from -3 to 3
- expand_weight: bfloat16 [1152, 4608], P('row', 'col'), may hold values from -0.1875 to 0.1875
- expand_offset: float32 [4608], P('col'), may hold values from -3 to 3
- shrink_weight: bfloat16 [4608, 1152], P('col', 'row'), may hold values from -0.09375 to 0.09375
- shrink_offset: float32 [1152], P('row'), may hold values from -3 to 3
- cotangent: bfloat16 [2048, 1152], P('col', 'row'), may hold values from -6 to 6
Outputs:
- result: bfloat16 [2048, 1152], P('col', 'row')
- hidden_grad: float32 [2048, 1152], P('col', 'row')
- caption_grad: float32 [1920, 1152], P('col', 'row')
- table_grad: float32 [6, 1152, 1000], P(None, 'row')
- shift_grad: float32 [6, 1152], P(None, 'row')
- query_grad: float32 [1152, 1152], P('row', 'col')
- key_grad: float32 [1152, 1152], P('row', 'col')
- value_grad: float32 [1152, 1152], P('row', 'col')
- output_grad: float32 [1152, 1152], P('col', 'row')
- probe_grad: float32 [1152, 1152], P('row', 'col')
- lookup_grad: float32 [1152, 1152], P('row', 'col')
- content_grad: float32 [1152, 1152], P('row', 'col')
- merge_grad: float32 [1152, 1152], P('col', 'row')
- expand_grad: float32 [1152, 4608], P('row', 'col')
- shrink_grad: float32 [4608, 1152], P('col', 'row')
- offset_query: float32 [1152], P('col')
- offset_value: float32 [1152], P('col')
- offset_output: float32 [1152], P('row')
- offset_probe: float32 [1152], P('col')
- offset_content: float32 [1152], P('col')
- offset_merge: float32 [1152], P('row')
- offset_expand: float32 [4608], P('col')
- offset_shrink: float32 [1152], P('row')
Inputs may be any that keep to these rules, and one draw needn't show every extreme that they name: `lengths`: the first latent has all 120 caption tokens and the second one has one.
All inputs are finite; a program needn't handle non-finite values.
Results may differ from a plain program's by a relative error of at most 0.023.
Values may be sent and summed in bfloat16 or wider, within the bound.
No kernel may reach another device: no remote copies, remote signals or barrier semaphores. Data moves between devices by JAX's collectives and lax.ppermute only.
A program may use at most 128 MiB of HBM per device.

v0:
```python
import jax
import jax.numpy as jnp
from jax import lax
from jax.sharding import PartitionSpec as P

D = 1152
HDIM = 72
LTXT = 120
LEN = 128
TSTEPS = 1000


EPSILON = 1e-06


def shortened(x):

    def short(part):
        return part.astype(jnp.bfloat16) if part.dtype == jnp.float32 else part

    return jax.tree.map(short, x)


def multiply(left_side, right_side):
    return jnp.dot(left_side, right_side, preferred_element_type=jnp.float32)


def multiply_back(left_side, right_side):
    return lax.dot_general(
        left_side, right_side, (((1,), (1,)), ((), ())), preferred_element_type=jnp.float32
    )


def multiply_outer(left_side, right_side):
    return lax.dot_general(
        left_side, right_side, (((0,), (0,)), ((), ())), preferred_element_type=jnp.float32
    )


def activate(values):
    return jax.nn.gelu(values, approximate=True)


def activate_back(values, upstream):
    return jax.vjp(activate, values)[1](upstream)[0]


def gather_cols(pieces):
    return jax.tree.map(
        lambda part, own: part.astype(own.dtype),
        lax.all_gather(shortened(pieces), "col", axis=0, tiled=True),
        pieces,
    )


def gather_rows(pieces):
    return jax.tree.map(
        lambda part, own: part.astype(own.dtype),
        lax.all_gather(shortened(pieces), "row", axis=0, tiled=True),
        pieces,
    )


def reduce_cols(partials):
    return lax.psum_scatter(partials, "col", scatter_dimension=0, tiled=True)


def project(sources, weights, owners, backward):
    product = multiply_back if backward else multiply
    partials = tuple((product(sources[owner], weight) for owner, weight in zip(owners, weights)))
    return lax.psum_scatter(partials, "row", scatter_dimension=0, tiled=True)


def feature_means(first_term, second_term):
    totals = lax.psum((jnp.sum(first_term, axis=1), jnp.sum(second_term, axis=1)), "row")
    return (totals[0][:, None] / D, totals[1][:, None] / D)


def normalize(values):
    center, squares = feature_means(values, values * values)
    factor = lax.rsqrt(squares - center * center + EPSILON)
    return ((values - center) * factor, factor)


def normalize_back(upstream, normed, factor):
    first_mean, second_mean = feature_means(upstream, upstream * normed)
    return factor * (upstream - first_mean - normed * second_mean)


def score_block(query_rows, key_rows, valid_keys):
    scores = jnp.einsum(
        "bqhe,bkhe->bhqk", query_rows, key_rows, preferred_element_type=jnp.float32
    ) * HDIM ** (-0.5)
    return jnp.where(valid_keys, scores, -1e30)


def attend(query_rows, key_rows, value_rows, valid_keys):
    scores = score_block(query_rows, key_rows, valid_keys)
    highest = jnp.max(scores, axis=-1, keepdims=True)
    logsum = highest + jnp.log(jnp.sum(jnp.exp(scores - highest), axis=-1, keepdims=True))
    soft_weights = jnp.exp(scores - logsum).astype(jnp.bfloat16)
    mixed_rows = jnp.einsum(
        "bhqk,bkhe->bqhe", soft_weights, value_rows, preferred_element_type=jnp.float32
    )
    return (mixed_rows.astype(jnp.bfloat16), logsum)


def attend_back(query_rows, key_rows, value_rows, valid_keys, logsum, upstream):
    soft_weights = jnp.exp(score_block(query_rows, key_rows, valid_keys) - logsum)
    value_grads = jnp.einsum(
        "bhqk,bqhe->bkhe",
        soft_weights.astype(jnp.bfloat16),
        upstream,
        preferred_element_type=jnp.float32,
    )
    weight_grads = jnp.einsum(
        "bqhe,bkhe->bhqk", upstream, value_rows, preferred_element_type=jnp.float32
    )
    inner_sum = jnp.sum(soft_weights * weight_grads, axis=-1, keepdims=True)
    score_grads = (soft_weights * (weight_grads - inner_sum) * HDIM ** (-0.5)).astype(jnp.bfloat16)
    query_grads = jnp.einsum(
        "bhqk,bkhe->bqhe", score_grads, key_rows, preferred_element_type=jnp.float32
    )
    key_grads = jnp.einsum(
        "bhqk,bqhe->bkhe", score_grads, query_rows, preferred_element_type=jnp.float32
    )
    return (query_grads, key_grads, value_grads)


def by_latent(values):
    return values.reshape(-1, LEN, values.shape[-1])


def flatten(values):
    return values.reshape(-1, values.shape[-1])


def by_head(values, length):
    return values.reshape(-1, length, values.shape[-1] // HDIM, HDIM)


def modulated(modulation, index):
    return modulation[:, index][:, None, :]


def token_sums(values):
    return jnp.sum(by_latent(values), axis=1)


def per_device(
    hidden,
    caption,
    lengths,
    timesteps,
    time_table,
    shift_table,
    query_weight,
    query_offset,
    key_weight,
    value_weight,
    value_offset,
    output_weight,
    output_offset,
    probe_weight,
    probe_offset,
    lookup_weight,
    content_weight,
    content_offset,
    merge_weight,
    merge_offset,
    expand_weight,
    expand_offset,
    shrink_weight,
    shrink_offset,
    cotangent,
):
    width_rows = hidden.shape[1]
    col_latents = hidden.shape[0] // LEN
    col_first = lax.axis_index("col") * col_latents
    step_slice = lax.dynamic_slice_in_dim(timesteps, col_first, col_latents)
    step_picks = (step_slice[:, None] == jnp.arange(TSTEPS, dtype=jnp.int32)[None, :]).astype(
        jnp.float32
    )
    modulation = (
        lax.dot_general(
            step_picks,
            time_table.reshape(6 * width_rows, TSTEPS),
            (((1,), (1,)), ((), ())),
            precision=lax.Precision.HIGHEST,
        ).reshape(col_latents, 6, width_rows)
        + shift_table[None]
    )
    start = hidden.astype(jnp.float32)
    normed_one, factor_one = normalize(start)
    attend_input = flatten(
        by_latent(normed_one) * (1.0 + modulated(modulation, 1)) + modulated(modulation, 0)
    ).astype(jnp.bfloat16)
    first_full = gather_cols((attend_input, caption))
    reduced = project(
        (first_full[0], first_full[1]),
        (query_weight, key_weight, value_weight, lookup_weight, content_weight),
        (0, 0, 0, 1, 1),
        False,
    )
    query_rows = (reduced[0] + query_offset).astype(jnp.bfloat16)
    key_rows = reduced[1].astype(jnp.bfloat16)
    value_rows = (reduced[2] + value_offset).astype(jnp.bfloat16)
    lookup_rows = reduced[3].astype(jnp.bfloat16)
    content_rows = (reduced[4] + content_offset).astype(jnp.bfloat16)
    row_latents = query_rows.shape[0] // LEN
    length_slice = lax.dynamic_slice_in_dim(
        lengths, lax.axis_index("row") * row_latents, row_latents
    )
    valid_text = (jnp.arange(LTXT, dtype=jnp.int32)[None, :] < length_slice[:, None])[
        :, None, None, :
    ]
    every_key = jnp.ones((1, 1, 1, 1), dtype=jnp.bool_)
    self_mixed, self_logsum = attend(
        by_head(query_rows, LEN), by_head(key_rows, LEN), by_head(value_rows, LEN), every_key
    )
    self_mixed = self_mixed.reshape(query_rows.shape)
    mixed_full = gather_rows(self_mixed)
    branch_self = reduce_cols(multiply(mixed_full, output_weight)) + output_offset
    after_self = start + flatten(modulated(modulation, 2) * by_latent(branch_self))
    cross_input = after_self.astype(jnp.bfloat16)
    cross_full = gather_cols(cross_input)
    probe_rows = (project((cross_full,), (probe_weight,), (0,), False)[0] + probe_offset).astype(
        jnp.bfloat16
    )
    cross_mixed, cross_logsum = attend(
        by_head(probe_rows, LEN),
        by_head(lookup_rows, LTXT),
        by_head(content_rows, LTXT),
        valid_text,
    )
    cross_mixed = cross_mixed.reshape(probe_rows.shape)
    cross_mixed_full = gather_rows(cross_mixed)
    branch_cross = reduce_cols(multiply(cross_mixed_full, merge_weight)) + merge_offset
    after_cross = after_self + branch_cross
    normed_two, factor_two = normalize(after_cross)
    feed_input = flatten(
        by_latent(normed_two) * (1.0 + modulated(modulation, 4)) + modulated(modulation, 3)
    ).astype(jnp.bfloat16)
    feed_full = gather_cols(feed_input)
    expanded = project((feed_full,), (expand_weight,), (0,), False)[0] + expand_offset
    activated = activate(expanded).astype(jnp.bfloat16)
    activated_full = gather_rows(activated)
    branch_feed = reduce_cols(multiply(activated_full, shrink_weight)) + shrink_offset
    result = (after_cross + flatten(modulated(modulation, 5) * by_latent(branch_feed))).astype(
        jnp.bfloat16
    )
    upstream = cotangent.astype(jnp.float32)
    gate_feed_grad = token_sums(upstream * branch_feed)
    feed_branch_grad = flatten(modulated(modulation, 5) * by_latent(upstream))
    feed_branch_full = gather_cols(feed_branch_grad.astype(jnp.bfloat16))
    activated_grad = project((feed_branch_full,), (shrink_weight,), (0,), True)[0]
    shrink_grad = multiply_outer(activated_full, feed_branch_full)
    expanded_grad = activate_back(expanded, activated_grad)
    expanded_full = gather_rows(expanded_grad.astype(jnp.bfloat16))
    feed_input_grad = reduce_cols(multiply_back(expanded_full, expand_weight))
    expand_grad = multiply_outer(feed_full, expanded_full)
    scale_feed_grad = token_sums(feed_input_grad * normed_two)
    shift_feed_grad = token_sums(feed_input_grad)
    cross_grad = upstream + normalize_back(
        flatten(by_latent(feed_input_grad) * (1.0 + modulated(modulation, 4))),
        normed_two,
        factor_two,
    )
    cross_grad_full = gather_cols(cross_grad.astype(jnp.bfloat16))
    cross_mixed_grad = project((cross_grad_full,), (merge_weight,), (0,), True)[0].astype(
        jnp.bfloat16
    )
    merge_grad = multiply_outer(cross_mixed_full, cross_grad_full)
    probe_grads, lookup_grads, content_grads = attend_back(
        by_head(probe_rows, LEN),
        by_head(lookup_rows, LTXT),
        by_head(content_rows, LTXT),
        valid_text,
        cross_logsum,
        by_head(cross_mixed_grad, LEN),
    )
    probe_grads = probe_grads.reshape(probe_rows.shape)
    lookup_grads = lookup_grads.reshape(lookup_rows.shape)
    content_grads = content_grads.reshape(content_rows.shape)
    cross_back_full = gather_rows(
        (
            probe_grads.astype(jnp.bfloat16),
            lookup_grads.astype(jnp.bfloat16),
            content_grads.astype(jnp.bfloat16),
        )
    )
    cross_back = reduce_cols(
        (
            multiply_back(cross_back_full[0], probe_weight),
            multiply_back(cross_back_full[1], lookup_weight)
            + multiply_back(cross_back_full[2], content_weight),
        )
    )
    caption_grad = cross_back[1]
    second_full = (cross_full, first_full[1])
    probe_grad = multiply_outer(second_full[0], cross_back_full[0])
    lookup_grad = multiply_outer(second_full[1], cross_back_full[1])
    content_grad = multiply_outer(second_full[1], cross_back_full[2])
    self_grad = cross_grad + cross_back[0]
    gate_self_grad = token_sums(self_grad * branch_self)
    self_branch_grad = flatten(modulated(modulation, 2) * by_latent(self_grad))
    self_branch_full = gather_cols(self_branch_grad.astype(jnp.bfloat16))
    self_mixed_grad = project((self_branch_full,), (output_weight,), (0,), True)[0].astype(
        jnp.bfloat16
    )
    output_grad = multiply_outer(mixed_full, self_branch_full)
    query_grads, key_grads, value_grads = attend_back(
        by_head(query_rows, LEN),
        by_head(key_rows, LEN),
        by_head(value_rows, LEN),
        every_key,
        self_logsum,
        by_head(self_mixed_grad, LEN),
    )
    query_grads = query_grads.reshape(query_rows.shape)
    key_grads = key_grads.reshape(key_rows.shape)
    value_grads = value_grads.reshape(value_rows.shape)
    self_back_full = gather_rows(
        (
            query_grads.astype(jnp.bfloat16),
            key_grads.astype(jnp.bfloat16),
            value_grads.astype(jnp.bfloat16),
        )
    )
    attend_input_grad = reduce_cols(
        multiply_back(self_back_full[0], query_weight)
        + multiply_back(self_back_full[1], key_weight)
        + multiply_back(self_back_full[2], value_weight)
    )
    attend_source = first_full[0]
    query_grad = multiply_outer(attend_source, self_back_full[0])
    key_grad = multiply_outer(attend_source, self_back_full[1])
    value_grad = multiply_outer(attend_source, self_back_full[2])
    scale_self_grad = token_sums(attend_input_grad * normed_one)
    shift_self_grad = token_sums(attend_input_grad)
    hidden_grad = self_grad + normalize_back(
        flatten(by_latent(attend_input_grad) * (1.0 + modulated(modulation, 1))),
        normed_one,
        factor_one,
    )
    modulation_grad = jnp.stack(
        [
            shift_self_grad,
            scale_self_grad,
            gate_self_grad,
            shift_feed_grad,
            scale_feed_grad,
            gate_feed_grad,
        ],
        axis=1,
    )
    offset_terms = jnp.stack(
        [
            jnp.sum(self_branch_grad, axis=0),
            jnp.sum(cross_grad, axis=0),
            jnp.sum(feed_branch_grad, axis=0),
        ],
        axis=0,
    )[None]
    stream_totals = (
        lax.all_gather(modulation_grad, "col", axis=0, tiled=True),
        lax.all_gather(offset_terms, "col", axis=0, tiled=True),
    )
    every_modulation = stream_totals[0]
    every_offset = jnp.sum(stream_totals[1], axis=0)
    every_picks = (timesteps[:, None] == jnp.arange(TSTEPS, dtype=jnp.int32)[None, :]).astype(
        jnp.float32
    )
    table_grad = lax.dot_general(
        every_modulation.reshape(every_modulation.shape[0], 6 * width_rows),
        every_picks,
        (((0,), (0,)), ((), ())),
        precision=lax.Precision.HIGHEST,
    ).reshape(6, width_rows, TSTEPS)
    shift_grad = jnp.sum(every_modulation, axis=0)
    col_totals = lax.psum(
        (
            jnp.sum(query_grads, axis=0),
            jnp.sum(value_grads, axis=0),
            jnp.sum(probe_grads, axis=0),
            jnp.sum(content_grads, axis=0),
            jnp.sum(expanded_grad, axis=0),
        ),
        "row",
    )
    return (
        result,
        hidden_grad,
        caption_grad,
        table_grad,
        shift_grad,
        query_grad,
        key_grad,
        value_grad,
        output_grad,
        probe_grad,
        lookup_grad,
        content_grad,
        merge_grad,
        expand_grad,
        shrink_grad,
        col_totals[0],
        col_totals[1],
        every_offset[0],
        col_totals[2],
        col_totals[3],
        every_offset[1],
        col_totals[4],
        every_offset[2],
    )


def solution(mesh):
    return jax.shard_map(
        per_device,
        mesh=mesh,
        in_specs=(
            P("col", "row"),
            P("col", "row"),
            P(),
            P(),
            P(None, "row", None),
            P(None, "row"),
            P("row", "col"),
            P("col"),
            P("row", "col"),
            P("row", "col"),
            P("col"),
            P("col", "row"),
            P("row"),
            P("row", "col"),
            P("col"),
            P("row", "col"),
            P("row", "col"),
            P("col"),
            P("col", "row"),
            P("row"),
            P("row", "col"),
            P("col"),
            P("col", "row"),
            P("row"),
            P("col", "row"),
        ),
        out_specs=(
            P("col", "row"),
            P("col", "row"),
            P("col", "row"),
            P(None, "row", None),
            P(None, "row"),
            P("row", "col"),
            P("row", "col"),
            P("row", "col"),
            P("col", "row"),
            P("row", "col"),
            P("row", "col"),
            P("row", "col"),
            P("col", "row"),
            P("row", "col"),
            P("col", "row"),
            P("col"),
            P("col"),
            P("row"),
            P("col"),
            P("col"),
            P("row"),
            P("col"),
            P("row"),
        ),
        check_vma=False,
    )
```

profile of v0, /device:TPU:9, one launch (start us, length us, event | category | flops | bytes accessed | tf_op | source)
XLA Modules:
  0.0 1852.4 jit_solution(11820438425164240196)
XLA Ops:
  20.1 106.3 %all-reduce.10 = (f32[1024]{0:T(1024)S(1)}, f32[1024]{0:T(1024)S(1)}, bf16[1920,576]{0,1:T(8,128)(2,1)}) all-reduce(f32[1024]{0:T(1024)S(1)} %get-tuple-element.30, f32[1024]{0:T(1024)S(1)} %get-tuple-element.29, f32[1920,576]{0,1:T(8,128)} %fusion.106), channel_id=1, replica_groups=mesh['row'=16,'col'=2] {'row'}, use_global_device_ids=true, to_apply=%region_3.0 | all-reduce | flops 1107968 | bytes 6651904 | tf_op jit(solution)/shard_map/psum | solution.py:75
  142.6 66.1 %reduce-scatter.24.cloned.1.call-done = f32[128,576]{0,1:T(8,128)} async-done(((f32[2048,576]{0,1:T(8,128)}), f32[128,576]{0,1:T(8,128)}) %reduce-scatter.24.cloned.1.call-update) | async-done | bytes 294928 | tf_op jit(solution)/shard_map/reduce_scatter | solution.py:71
  209.6 77.7 %reduce-scatter.22.cloned.1.call-done = f32[128,576]{0,1:T(8,128)} async-done(((f32[2048,576]{0,1:T(8,128)}), f32[128,576]{0,1:T(8,128)}) %reduce-scatter.22.cloned.1.call-update) | async-done | bytes 294928 | tf_op jit(solution)/shard_map/reduce_scatter | solution.py:71
  289.1 76.9 %reduce-scatter.20.cloned.1.call-done = f32[128,576]{0,1:T(8,128)} async-done(((f32[2048,576]{0,1:T(8,128)}), f32[128,576]{0,1:T(8,128)}) %reduce-scatter.20.cloned.1.call-update) | async-done | bytes 294928 | tf_op jit(solution)/shard_map/reduce_scatter | solution.py:71
  368.1 43.8 %all-gather.16.cloned.1.call-done = bf16[2048,576]{0,1:T(8,128)(2,1)} async-done(((bf16[128,576]{0,1:T(8,128)(2,1)}), bf16[2048,576]{0,1:T(8,128)(2,1)}) %all-gather.16.cloned.1.call-update) | async-done | bytes 2359312 | tf_op jit(solution)/shard_map/all_gather | solution.py:59
  418.1 11.3 reduce-scatter.26.cloned.1.call-done
  443.1 101.8 %all-reduce.9.cloned.1.call-done = f32[1920,576]{0,1:T(8,128)} async-done(((f32[1920,576]{0,1:T(8,128)}), f32[1920,576]{0,1:T(8,128)}) %all-reduce.9.cloned.1.call-update) | async-done | bytes 4423696
  546.2 76.7 %reduce-scatter.28.cloned.1.call-done = f32[128,576]{0,1:T(8,128)} async-done(((f32[2048,576]{0,1:T(8,128)}), f32[128,576]{0,1:T(8,128)}) %reduce-scatter.28.cloned.1.call-update) | async-done | bytes 294928 | tf_op jit(solution)/shard_map/reduce_scatter | solution.py:71
  626.2 43.3 %all-gather.18.cloned.1.call-done = bf16[2048,576]{0,1:T(8,128)(2,1)} async-done(((bf16[128,576]{0,1:T(8,128)(2,1)}), bf16[2048,576]{0,1:T(8,128)(2,1)}) %all-gather.18.cloned.1.call-update) | async-done | bytes 2359312 | tf_op jit(solution)/shard_map/all_gather | solution.py:59
  679.6 8.0 fusion.110
  690.2 25.1 %all-reduce.4 = (f32[1024]{0:T(1024)S(1)}, f32[1024]{0:T(1024)S(1)}) all-reduce(f32[1024]{0:T(1024)S(1)} %get-tuple-element.28, f32[1024]{0:T(1024)S(1)} %get-tuple-element.27), channel_id=1, replica_groups=mesh['row'=16,'col'=2] {'row'}, use_global_device_ids=true, to_apply=%region_19.20 | all-reduce | flops 2048 | bytes 16384 | tf_op jit(solution)/shard_map/psum | solution.py:75
  723.6 9.2 fusion.108
  732.9 150.9 %reduce-scatter.36.cloned.1.call-done = f32[128,2304]{1,0:T(8,128)} async-done(((f32[2048,2304]{1,0:T(8,128)}), f32[128,2304]{1,0:T(8,128)}) %reduce-scatter.36.cloned.1.call-update) | async-done | bytes 1179664 | tf_op jit(solution)/shard_map/reduce_scatter | solution.py:71
  883.8 197.3 %reduce-scatter.32.cloned.1.call-done = f32[128,2304]{1,0:T(8,128)} async-done(((f32[2048,2304]{1,0:T(8,128)}), f32[128,2304]{1,0:T(8,128)}) %reduce-scatter.32.cloned.1.call-update) | async-done | bytes 1179664 | tf_op jit(solution)/shard_map/reduce_scatter | solution.py:71
  1085.4 80.7 %all-gather.22.cloned.1.call-done = bf16[2048,2304]{1,0:T(8,128)(2,1)} async-done(((bf16[128,2304]{1,0:T(8,128)(2,1)}), bf16[2048,2304]{1,0:T(8,128)(2,1)}) %all-gather.22.cloned.1.call-update) | async-done | bytes 9437200 | tf_op jit(solution)/shard_map/all_gather | solution.py:59
  1166.2 7.4 fusion.111
  1173.7 74.7 %all-gather.20.cloned.1.call-done = bf16[2048,2304]{1,0:T(8,128)(2,1)} async-done(((bf16[128,2304]{1,0:T(8,128)(2,1)}), bf16[2048,2304]{1,0:T(8,128)(2,1)}) %all-gather.20.cloned.1.call-update) | async-done | bytes 9437200 | tf_op jit(solution)/shard_map/all_gather | solution.py:59
  1248.4 7.4 fusion.109
  1255.9 8.9 reduce-scatter.38.cloned.1.call-done
  1265.9 23.6 %all-reduce.3 = (f32[1024]{0:T(1024)S(1)}, f32[1024]{0:T(1024)}) all-reduce(f32[1024]{0:T(1024)S(1)} %get-tuple-element.26, f32[1024]{0:T(1024)S(1)} %get-tuple-element.25), channel_id=1, replica_groups=mesh['row'=16,'col'=2] {'row'}, use_global_device_ids=true, to_apply=%region_27.28 | all-reduce | flops 2048 | bytes 16384 | tf_op jit(solution)/shard_map/psum | solution.py:75
  1301.1 81.6 %reduce-scatter.40.cloned.1.call-done = f32[128,576]{0,1:T(8,128)} async-done(((f32[2048,576]{0,1:T(8,128)}), f32[128,576]{0,1:T(8,128)}) %reduce-scatter.40.cloned.1.call-update) | async-done | bytes 294928 | tf_op jit(solution)/shard_map/reduce_scatter | solution.py:71
  1387.1 43.4 %all-gather.24.cloned.1.call-done = bf16[2048,576]{0,1:T(8,128)(2,1)} async-done(((bf16[128,576]{0,1:T(8,128)(2,1)}), bf16[2048,576]{0,1:T(8,128)(2,1)}) %all-gather.24.cloned.1.call-update) | async-done | bytes 2359312 | tf_op jit(solution)/shard_map/all_gather | solution.py:59
  1438.0 10.1 reduce-scatter.42.cloned.1.call-done
  1457.8 35.3 %all-gather.34.cloned.1.call-done = bf16[16,120,576]{1,2,0:T(8,128)(2,1)} async-done(((bf16[1,120,576]{1,2,0:T(8,128)(2,1)}), bf16[16,120,576]{1,2,0:T(8,128)(2,1)}) %all-gather.34.cloned.1.call-update) | async-done | bytes 2211856 | tf_op jit(solution)/shard_map/all_gather | solution.py:59
  1503.1 33.8 %all-gather.32.cloned.1.call-done = bf16[16,120,576]{1,2,0:T(8,128)(2,1)} async-done(((bf16[1,120,576]{1,2,0:T(8,128)(2,1)}), bf16[16,120,576]{1,2,0:T(8,128)(2,1)}) %all-gather.32.cloned.1.call-update) | async-done | bytes 2211856 | tf_op jit(solution)/shard_map/all_gather | solution.py:59
  1553.4 59.6 %reduce-scatter.44.cloned.1.call-done = f32[128,576]{0,1:T(8,128)} async-done(((f32[2048,576]{0,1:T(8,128)}), f32[128,576]{0,1:T(8,128)}) %reduce-scatter.44.cloned.1.call-update) | async-done | bytes 294928 | tf_op jit(solution)/shard_map/reduce_scatter | solution.py:71
  1621.0 6.6 fusion.126
  1627.5 6.4 fusion.125
  1652.1 29.6 %all-gather.26.cloned.1.call-done = bf16[2048,576]{0,1:T(8,128)(2,1)} async-done(((bf16[128,576]{0,1:T(8,128)(2,1)}), bf16[2048,576]{0,1:T(8,128)(2,1)}) %all-gather.26.cloned.1.call-update) | async-done | bytes 2359312 | tf_op jit(solution)/shard_map/all_gather | solution.py:59
  1683.9 41.3 %all-gather.28.cloned.1.call-done = bf16[2048,576]{0,1:T(8,128)(2,1)} async-done(((bf16[128,576]{0,1:T(8,128)(2,1)}), bf16[2048,576]{0,1:T(8,128)(2,1)}) %all-gather.28.cloned.1.call-update) | async-done | bytes 2359312 | tf_op jit(solution)/shard_map/all_gather | solution.py:59
  1727.4 41.4 %all-gather.30.cloned.1.call-done = bf16[2048,576]{0,1:T(8,128)(2,1)} async-done(((bf16[128,576]{0,1:T(8,128)(2,1)}), bf16[2048,576]{0,1:T(8,128)(2,1)}) %all-gather.30.cloned.1.call-update) | async-done | bytes 2359312 | tf_op jit(solution)/shard_map/all_gather | solution.py:59
  1787.4 48.9 %all-reduce.2 = (f32[1024]{0:T(1024)S(1)}, f32[1024]{0:T(1024)S(1)}, f32[576]{0:T(1024)}, f32[576]{0:T(1024)}, f32[576]{0:T(1024)}, /*index=5*/f32[576]{0:T(1024)}, f32[2304]{0:T(1024)}) all-reduce(f32[1024]{0:T(1024)S(1)} %get-tuple-element.24, f32[1024]{0:T(1024)S(1)} %get-tuple-element.23, ...), channel_id=1, replica_groups=mesh['row'=16,'col'=2] {'row'}, use_global_device_ids=true, to_apply=%region_37.38 | all-reduce | flops 6656 | bytes 53248 | tf_op jit(solution)/shard_map/psum | solution.py:75
  (312 shorter events, 201.4 us)
Async XLA Ops:
  7.2 201.4 %reduce-scatter.24.cloned.1.call-start = ((), (), s32[]{:S(2)}) async-start(), calls=%async_computation.17 | async-start | bytes 5013504 | tf_op jit(solution)/shard_map/reduce_scatter | solution.py:71
  134.8 152.5 %reduce-scatter.22.cloned.1.call-start = ((), (), s32[]{:S(2)}) async-start(), calls=%async_computation.16 | async-start | bytes 5013504 | tf_op jit(solution)/shard_map/reduce_scatter | solution.py:71
  138.7 227.4 %reduce-scatter.20.cloned.1.call-start = ((), (), s32[]{:S(2)}) async-start(), calls=%async_computation.15 | async-start | bytes 5013504 | tf_op jit(solution)/shard_map/reduce_scatter | solution.py:71
  142.5 223.5 %copy-start.51 = (f32[576]{0:T(1024)S(1)}, f32[576]{0:T(1024)}, u32[]{:S(2)}) copy-start(f32[576]{0:T(1024)} %param.35) | copy-start | bytes 6916
  142.5 269.4 %copy-start.35 = (bf16[576,72]{0,1:T(8,128)(2,1)S(1)}, bf16[576,72]{0,1:T(8,128)(2,1)}, u32[]{:S(2)}) copy-start(bf16[576,72]{0,1:T(8,128)(2,1)} %param.36) | copy-start | bytes 248836
  142.5 269.4 %all-gather.16.cloned.1.call-start = ((), (), s32[]{:S(2)}) async-start(), calls=%async_computation.18 | async-start | bytes 2506752 | tf_op jit(solution)/shard_map/all_gather | solution.py:59
  209.6 205.3 %copy-start.28 = (bf16[128,576]{0,1:T(8,128)(2,1)}, bf16[128,576]{0,1:T(8,128)(2,1)S(1)}, u32[]{:S(2)}) copy-start(bf16[128,576]{0,1:T(8,128)(2,1)S(1)} %convert_element_type.147) | copy-start | bytes 442372
  368.1 61.3 %reduce-scatter.26.cloned.1.call-start = ((), (), s32[]{:S(2)}) async-start(), calls=%async_computation.19 | async-start | bytes 884736 | tf_op jit(solution)/shard_map/reduce_scatter | solution.py:65
  415.0 129.9 %all-reduce.9.cloned.1.call-start = ((), (), s32[]{:S(2)}) async-start(), calls=%async_computation.40 | async-start | bytes 8847360
  418.0 205.0 %reduce-scatter.28.cloned.1.call-start = ((), (), s32[]{:S(2)}) async-start(), calls=%async_computation.20 | async-start | bytes 5013504 | tf_op jit(solution)/shard_map/reduce_scatter | solution.py:71
  438.9 184.1 %copy-start.53 = (f32[576]{0:T(1024)S(1)}, f32[576]{0:T(1024)}, u32[]{:S(2)}) copy-start(f32[576]{0:T(1024)} %param.39) | copy-start | bytes 6916
  438.9 230.6 %copy-start.32 = (bf16[576,72]{0,1:T(8,128)(2,1)S(1)}, bf16[576,72]{0,1:T(8,128)(2,1)}, u32[]{:S(2)}) copy-start(bf16[576,72]{0,1:T(8,128)(2,1)} %param.43) | copy-start | bytes 248836
  438.9 230.6 %all-gather.18.cloned.1.call-start = ((), (), s32[]{:S(2)}) async-start(), calls=%async_computation.21 | async-start | bytes 2506752 | tf_op jit(solution)/shard_map/all_gather | solution.py:59
  626.2 62.9 %reduce-scatter.30.cloned.1.call-start = ((), (), s32[]{:S(2)}) async-start(), calls=%async_computation.22 | async-start | bytes 884736 | tf_op jit(solution)/shard_map/reduce_scatter | solution.py:65
  672.6 211.2 %reduce-scatter.36.cloned.1.call-start = ((), (), s32[]{:S(2)}) async-start(), calls=%async_computation.26 | async-start | bytes 20054016 | tf_op jit(solution)/shard_map/reduce_scatter | solution.py:71
  687.6 393.5 %reduce-scatter.32.cloned.1.call-start = ((), (), s32[]{:S(2)}) async-start(), calls=%async_computation.23 | async-start | bytes 20054016 | tf_op jit(solution)/shard_map/reduce_scatter | solution.py:71
  732.8 348.3 %copy-start.47 = (f32[2304]{0:T(1024)S(1)}, f32[2304]{0:T(1024)}, u32[]{:S(2)}) copy-start(f32[2304]{0:T(1024)} %param.46) | copy-start | bytes 27652
  732.8 433.4 %all-gather.22.cloned.1.call-start = ((), (), s32[]{:S(2)}) async-start(), calls=%async_computation.27 | async-start | bytes 10027008 | tf_op jit(solution)/shard_map/all_gather | solution.py:59
  1084.6 163.8 %all-gather.20.cloned.1.call-start = ((), (), s32[]{:S(2)}) async-start(), calls=%async_computation.24 | async-start | bytes 10027008 | tf_op jit(solution)/shard_map/all_gather | solution.py:59
  1085.4 179.4 %reduce-scatter.38.cloned.1.call-start = ((), (), s32[]{:S(2)}) async-start(), calls=%async_computation.28 | async-start | bytes 884736 | tf_op jit(solution)/shard_map/reduce_scatter | solution.py:65
  1173.6 116.5 %reduce-scatter.34.cloned.1.call-start = ((), (), s32[]{:S(2)}) async-start(), calls=%async_computation.25 | async-start | bytes 884736 | tf_op jit(solution)/shard_map/reduce_scatter | solution.py:65
  1255.8 126.8 %reduce-scatter.40.cloned.1.call-start = ((), (), s32[]{:S(2)}) async-start(), calls=%async_computation.29 | async-start | bytes 5013504 | tf_op jit(solution)/shard_map/reduce_scatter | solution.py:71
  1301.0 129.5 %all-gather.24.cloned.1.call-start = ((), (), s32[]{:S(2)}) async-start(), calls=%async_computation.30 | async-start | bytes 2506752 | tf_op jit(solution)/shard_map/all_gather | solution.py:59
  1387.1 61.0 %reduce-scatter.42.cloned.1.call-start = ((), (), s32[]{:S(2)}) async-start(), calls=%async_computation.31 | async-start | bytes 884736 | tf_op jit(solution)/shard_map/reduce_scatter | solution.py:65
  1433.6 59.5 %all-gather.34.cloned.1.call-start = ((), (), s32[]{:S(2)}) async-start(), calls=%async_computation.38 | async-start | bytes 2506752 | tf_op jit(solution)/shard_map/all_gather | solution.py:59
  1435.6 101.3 %all-gather.32.cloned.1.call-start = ((), (), s32[]{:S(2)}) async-start(), calls=%async_computation.37 | async-start | bytes 2506752 | tf_op jit(solution)/shard_map/all_gather | solution.py:59
  1437.9 175.1 %reduce-scatter.44.cloned.1.call-start = ((), (), s32[]{:S(2)}) async-start(), calls=%async_computation.32 | async-start | bytes 5013504 | tf_op jit(solution)/shard_map/reduce_scatter | solution.py:71
  1457.5 188.5 %reduce-scatter.48.cloned.1.call-start = ((), (), s32[]{:S(2)}) async-start(), calls=%async_computation.39 | async-start | bytes 1474560
  1553.3 128.3 %all-gather.26.cloned.1.call-start = ((), (), s32[]{:S(2)}) async-start(), calls=%async_computation.33 | async-start | bytes 2506752 | tf_op jit(solution)/shard_map/all_gather | solution.py:59
  1617.3 107.8 %all-gather.28.cloned.1.call-start = ((), (), s32[]{:S(2)}) async-start(), calls=%async_computation.34 | async-start | bytes 2506752 | tf_op jit(solution)/shard_map/all_gather | solution.py:59
  1619.6 149.2 %all-gather.30.cloned.1.call-start = ((), (), s32[]{:S(2)}) async-start(), calls=%async_computation.35 | async-start | bytes 2506752 | tf_op jit(solution)/shard_map/all_gather | solution.py:59
  1620.7 165.6 %reduce-scatter.46.cloned.1.call-start = ((), (), s32[]{:S(2)}) async-start(), calls=%async_computation.36 | async-start | bytes 884736 | tf_op jit(solution)/shard_map/reduce_scatter | solution.py:65
  (53 other events, 1816.0 us)
Sparse Core Ops, SparseCore 0:
  134.9 73.6 reduce-scatter.23
  212.5 74.7 reduce-scatter.21
  291.2 74.7 reduce-scatter.19
  368.6 43.2 all-gather.15
  415.1 14.2 reduce-scatter.25
  433.0 111.9 all-reduce.8
  548.8 74.1 reduce-scatter.27
  626.3 43.2 all-gather.17
  672.7 14.7 reduce-scatter.29
  691.4 192.2 reduce-scatter.35
  887.9 193.1 reduce-scatter.31
  1084.7 81.3 all-gather.21
  1169.0 79.3 all-gather.19
  1251.1 13.6 reduce-scatter.37
  1267.5 15.3 reduce-scatter.33
  1301.1 81.4 reduce-scatter.39
  1387.2 43.2 all-gather.23
  1433.7 14.2 reduce-scatter.41
  1450.9 42.1 all-gather.33
  1495.8 41.0 all-gather.31
  1540.7 72.2 reduce-scatter.43
  1615.9 20.9 reduce-scatter.47
  1639.6 41.9 all-gather.25
  1684.2 40.8 all-gather.27
  1727.9 40.8 all-gather.29
  1772.0 14.2 reduce-scatter.45
where the time goes:
time: 1880 us; the launch traced here: 1850 us
  waiting for transfers between devices  1390 us (74%)
  blocking collectives  249 us (13%)
  matrix products  132 us (7%)
  local copies, waits for them, and re-layouts  38 us (2%)
  other arithmetic  26.1 us (1%)
    reduce_scatter x8, waiting for transfers between devices, project(): return lax.psum_scatter(partials, 'row', scatter_dimension=0, tiled=True)  787 us
    all_gather x10, waiting for transfers between devices, gather_rows(): lax.all_gather(shortened(pieces), 'row', axis=0, tiled=True)  467 us
    psum x4, blocking collectives, feature_means(): lax.psum((jnp.sum(first_term, axis=1), jnp.sum(second_term, axis=1)), 'row')  204 us
    unnamed x28, waiting for transfers between devices  103 us
    dot_general x10, matrix products, multiply(): return jnp.dot(left_side, right_side, preferred_element_type=jnp.float32)  40.4 us
    all_gather x7, blocking collectives, gather_cols(): lax.all_gather(shortened(pieces), 'col', axis=0, tiled=True)  37.9 us
  transfers between devices with their start and end apart: 26, of which 23 were waited for; matrix products, arithmetic and copies ran while one was open for 8% of the time, Pallas kernels for 0%

commit v1 on v0

v1 whole, which is shorter than its diff:
```python
import jax
import jax.numpy as jnp
from jax import lax
from jax.sharding import PartitionSpec as P

D = 1152
HDIM = 72
LTXT = 120
LEN = 128
TSTEPS = 1000


EPSILON = 1e-06


def multiply(left_side, right_side):
    return jnp.dot(left_side, right_side, preferred_element_type=jnp.float32)


def multiply_back(left_side, right_side):
    return lax.dot_general(
        left_side, right_side, (((1,), (1,)), ((), ())), preferred_element_type=jnp.float32
    )


def multiply_outer(left_side, right_side):
    return lax.dot_general(
        left_side, right_side, (((0,), (0,)), ((), ())), preferred_element_type=jnp.float32
    )


def activate(values):
    return jax.nn.gelu(values, approximate=True)


def activate_back(values, upstream):
    return jax.vjp(activate, values)[1](upstream)[0]


def score_block(query_rows, key_rows, valid_keys):
    scores = jnp.einsum(
        "bqhe,bkhe->bhqk", query_rows, key_rows, preferred_element_type=jnp.float32
    ) * HDIM ** (-0.5)
    return jnp.where(valid_keys, scores, -1e30)


def attend(query_rows, key_rows, value_rows, valid_keys):
    scores = score_block(query_rows, key_rows, valid_keys)
    highest = jnp.max(scores, axis=-1, keepdims=True)
    logsum = highest + jnp.log(jnp.sum(jnp.exp(scores - highest), axis=-1, keepdims=True))
    soft_weights = jnp.exp(scores - logsum).astype(jnp.bfloat16)
    mixed_rows = jnp.einsum(
        "bhqk,bkhe->bqhe", soft_weights, value_rows, preferred_element_type=jnp.float32
    )
    return (mixed_rows.astype(jnp.bfloat16), logsum)


def attend_back(query_rows, key_rows, value_rows, valid_keys, logsum, upstream):
    soft_weights = jnp.exp(score_block(query_rows, key_rows, valid_keys) - logsum)
    value_grads = jnp.einsum(
        "bhqk,bqhe->bkhe",
        soft_weights.astype(jnp.bfloat16),
        upstream,
        preferred_element_type=jnp.float32,
    )
    weight_grads = jnp.einsum(
        "bqhe,bkhe->bhqk", upstream, value_rows, preferred_element_type=jnp.float32
    )
    inner_sum = jnp.sum(soft_weights * weight_grads, axis=-1, keepdims=True)
    score_grads = (soft_weights * (weight_grads - inner_sum) * HDIM ** (-0.5)).astype(jnp.bfloat16)
    query_grads = jnp.einsum(
        "bhqk,bkhe->bqhe", score_grads, key_rows, preferred_element_type=jnp.float32
    )
    key_grads = jnp.einsum(
        "bhqk,bqhe->bkhe", score_grads, query_rows, preferred_element_type=jnp.float32
    )
    return (query_grads, key_grads, value_grads)


LANES = 128


def padded(values):
    return jnp.pad(values, ((0, 0), (0, -values.shape[1] % LANES)))


def pack(pieces):
    starts = []
    width = 0
    blocks = []
    for piece in pieces:
        blocks.append(padded(piece))
        starts.append((width, width + piece.shape[1]))
        width += blocks[-1].shape[1]
    return (jnp.concatenate(blocks, axis=1), starts)


def unpack(packed, starts):
    return [packed[:, low:high] for low, high in starts]


def gather_rows(values):
    return lax.all_gather(values, "row", axis=0, tiled=True)


def col_sum(partial):
    if lax.axis_size("col") == 2:
        other = lax.ppermute(partial.astype(jnp.bfloat16), "col", [(0, 1), (1, 0)])
        return partial + other.astype(jnp.float32)
    return lax.psum(partial, "col")


def two_parts(values):
    high = values.astype(jnp.bfloat16)
    low = (values - high.astype(jnp.float32)).astype(jnp.bfloat16)
    return (high, low)


def feature_mean(values):
    return jnp.sum(values, axis=-1, keepdims=True) / D


def normalize(values):
    center = feature_mean(values)
    factor = lax.rsqrt(feature_mean(values * values) - center * center + EPSILON)
    return ((values - center) * factor, factor)


def normalize_back(upstream, normed, factor):
    return factor * (upstream - feature_mean(upstream) - normed * feature_mean(upstream * normed))


def by_head(values, length):
    return values.reshape(-1, length, values.shape[-1] // HDIM, HDIM)


def flat(values):
    return values.reshape(-1, values.shape[-1])


def to_token_rows(values):
    size = lax.axis_size("row")
    moved = lax.all_to_all(values, "row", 0, 0, tiled=True)
    moved = moved.reshape(size, -1, *moved.shape[1:]).transpose(1, 2, 0, 3)
    return moved.reshape(*moved.shape[:2], -1)


def to_features(values):
    size = lax.axis_size("row")
    own, rows, width = values.shape
    parts = values.reshape(own, rows, size, width // size).transpose(2, 0, 1, 3)
    return lax.all_to_all(parts.reshape(size * own, rows, -1), "row", 0, 0, tiled=True)


def outer_with_sum(sources, upstream):
    width = sources.shape[1]
    ones = jnp.ones((sources.shape[0], 1), jnp.bfloat16)
    wide = jnp.concatenate([sources, ones], axis=1)
    product = multiply_outer(jnp.pad(wide, ((0, 0), (0, -wide.shape[1] % 8))), upstream)
    return (product[:width], product[width])


def per_device(
    hidden,
    caption,
    lengths,
    timesteps,
    time_table,
    shift_table,
    query_weight,
    query_offset,
    key_weight,
    value_weight,
    value_offset,
    output_weight,
    output_offset,
    probe_weight,
    probe_offset,
    lookup_weight,
    content_weight,
    content_offset,
    merge_weight,
    merge_offset,
    expand_weight,
    expand_offset,
    shrink_weight,
    shrink_offset,
    cotangent,
):
    low = jnp.bfloat16
    width = hidden.shape[1]
    heads_width = query_weight.shape[1]
    latents = timesteps.shape[0]
    own = latents // lax.axis_size("row")
    col_latents = hidden.shape[0] // LEN

    near_pack, near_starts = pack(
        [
            jnp.concatenate([query_weight, key_weight, value_weight], axis=1),
            output_weight.T,
            probe_weight,
            jnp.concatenate([lookup_weight, content_weight], axis=1),
            merge_weight.T,
        ]
    )
    far_pack, far_starts = pack([expand_weight, shrink_weight.T])
    near_full = gather_rows(near_pack)

    picks = (timesteps[:, None] == jnp.arange(TSTEPS, dtype=jnp.int32)[None, :]).astype(
        jnp.float32
    )
    own_modulation = (
        lax.dot_general(
            picks,
            time_table.reshape(6 * width, TSTEPS),
            (((1,), (1,)), ((), ())),
            precision=lax.Precision.HIGHEST,
        ).reshape(latents, 6, width)
        + shift_table[None]
    )
    whole = lax.all_gather(
        jnp.concatenate([hidden, cotangent, caption], axis=0), "col", axis=0, tiled=False
    )
    tokens = hidden.shape[0]
    hidden_all = whole[:, :tokens].reshape(latents, LEN, width)
    cotangent_all = whole[:, tokens : 2 * tokens].reshape(latents, LEN, width)
    caption_all = whole[:, 2 * tokens :].reshape(latents, LTXT, width)
    offsets = jnp.stack([output_offset, merge_offset, shrink_offset])[None]
    small = jnp.concatenate([own_modulation, jnp.broadcast_to(offsets, (latents, 3, width))], axis=1)
    arrived = to_token_rows(
        jnp.concatenate([hidden_all, cotangent_all, caption_all, *two_parts(small)], axis=1)
    )
    far_pack, arrived = lax.optimization_barrier((far_pack, arrived))
    far_full = gather_rows(far_pack)

    start = flat(arrived[:, :LEN]).astype(jnp.float32)
    upstream = flat(arrived[:, LEN : 2 * LEN]).astype(jnp.float32)
    text = flat(arrived[:, 2 * LEN : 2 * LEN + LTXT])
    tail = arrived[:, 2 * LEN + LTXT :].astype(jnp.float32)
    modulation = tail[:, :9] + tail[:, 9:]
    output_bias, merge_bias, shrink_bias = (modulation[0, 6 + i][None] for i in range(3))

    def spread(index):
        rows = jnp.broadcast_to(modulation[:, index][:, None], (own, LEN, D))
        return flat(rows)

    def latent_sums(values):
        return jnp.sum(values.reshape(own, LEN, -1), axis=1)

    shift_a, scale_a, gate_a, shift_f, scale_f, gate_f = (spread(i) for i in range(6))
    qkv_weight, output_flip, probe_full, text_weight, merge_flip = unpack(near_full, near_starts)
    expand_full, shrink_flip = unpack(far_full, far_starts)

    normed_one, factor_one = normalize(start)
    attend_input = (normed_one * (1.0 + scale_a) + shift_a).astype(low)
    no_offset = jnp.zeros_like(query_offset)
    qkv_rows = (
        multiply(attend_input, qkv_weight)
        + jnp.concatenate([query_offset, no_offset, value_offset])[None]
    ).astype(low)
    query_rows, key_rows, value_rows = (
        by_head(qkv_rows[:, i * heads_width : (i + 1) * heads_width], LEN) for i in range(3)
    )
    text_rows = (
        multiply(text, text_weight) + jnp.concatenate([no_offset, content_offset])[None]
    ).astype(low)
    lookup_rows = by_head(text_rows[:, :heads_width], LTXT)
    content_rows = by_head(text_rows[:, heads_width:], LTXT)
    own_lengths = lax.dynamic_slice_in_dim(lengths, lax.axis_index("row") * own, own)
    valid_text = (jnp.arange(LTXT, dtype=jnp.int32)[None, :] < own_lengths[:, None])[
        :, None, None, :
    ]
    every_key = jnp.ones((1, 1, 1, 1), dtype=jnp.bool_)
    self_mixed, self_logsum = attend(query_rows, key_rows, value_rows, every_key)
    self_mixed = self_mixed.reshape(-1, heads_width)
    branch_self = col_sum(multiply_back(self_mixed, output_flip)) + output_bias
    after_self = start + gate_a * branch_self
    cross_input = after_self.astype(low)
    probe_rows = by_head((multiply(cross_input, probe_full) + probe_offset).astype(low), LEN)
    cross_mixed, cross_logsum = attend(probe_rows, lookup_rows, content_rows, valid_text)
    cross_mixed = cross_mixed.reshape(-1, heads_width)
    branch_cross = col_sum(multiply_back(cross_mixed, merge_flip)) + merge_bias
    after_cross = after_self + branch_cross
    normed_two, factor_two = normalize(after_cross)
    feed_input = (normed_two * (1.0 + scale_f) + shift_f).astype(low)
    expanded = multiply(feed_input, expand_full) + expand_offset
    activated = activate(expanded).astype(low)
    first_pack, first_starts = pack([activated, self_mixed, cross_mixed])
    first_full = gather_rows(first_pack)

    feed_branch_grad = gate_f * upstream
    activated_grad = multiply(feed_branch_grad.astype(low), shrink_flip)
    expanded_grad = activate_back(expanded, activated_grad).astype(low)
    feed_input_grad = col_sum(multiply_back(expanded_grad, expand_full))
    cross_grad = upstream + normalize_back(
        feed_input_grad * (1.0 + scale_f), normed_two, factor_two
    )
    cross_low = cross_grad.astype(low)
    cross_mixed_grad = multiply(cross_low, merge_flip).astype(low)
    probe_grads, lookup_grads, content_grads = attend_back(
        probe_rows,
        lookup_rows,
        content_rows,
        valid_text,
        cross_logsum,
        by_head(cross_mixed_grad, LEN),
    )
    probe_grads = probe_grads.reshape(-1, heads_width).astype(low)
    text_grads = jnp.concatenate(
        [lookup_grads.reshape(-1, heads_width), content_grads.reshape(-1, heads_width)], axis=1
    ).astype(low)
    self_grad = cross_grad + col_sum(multiply_back(probe_grads, probe_full))
    self_branch_grad = gate_a * self_grad
    self_branch_low = self_branch_grad.astype(low)
    self_mixed_grad = multiply(self_branch_low, output_flip).astype(low)
    qkv_grads = attend_back(
        query_rows, key_rows, value_rows, every_key, self_logsum, by_head(self_mixed_grad, LEN)
    )
    qkv_grads = jnp.concatenate(
        [part.reshape(-1, heads_width).astype(low) for part in qkv_grads], axis=1
    )
    text_wide = jnp.pad(text_grads.reshape(own, LTXT, -1), ((0, 0), (0, LEN - LTXT), (0, 0)))
    second_pack, second_starts = pack([expanded_grad, qkv_grads, probe_grads, flat(text_wide)])
    second_full = gather_rows(second_pack)

    branch_feed = col_sum(multiply_back(activated, shrink_flip)) + shrink_bias
    result = after_cross + gate_f * branch_feed
    caption_grad = col_sum(multiply_back(text_grads, text_weight))
    attend_input_grad = col_sum(multiply_back(qkv_grads, qkv_weight))
    hidden_grad = self_grad + normalize_back(
        attend_input_grad * (1.0 + scale_a), normed_one, factor_one
    )
    modulation_grad = jnp.stack(
        [
            latent_sums(attend_input_grad),
            latent_sums(attend_input_grad * normed_one),
            latent_sums(self_grad * branch_self),
            latent_sums(feed_input_grad),
            latent_sums(feed_input_grad * normed_two),
            latent_sums(upstream * branch_feed),
        ],
        axis=1,
    )

    def rows_of(values, length):
        return values.astype(low).reshape(own, length, D)

    returned = to_features(
        jnp.concatenate(
            [
                rows_of(result, LEN),
                rows_of(hidden_grad, LEN),
                rows_of(attend_input, LEN),
                rows_of(cross_input, LEN),
                rows_of(feed_input, LEN),
                rows_of(cross_grad, LEN),
                rows_of(self_branch_grad, LEN),
                rows_of(caption_grad, LTXT),
                *two_parts(modulation_grad),
            ],
            axis=1,
        )
    )
    col_first = lax.axis_index("col") * col_latents
    here = lax.dynamic_slice_in_dim(returned, col_first, col_latents)
    features = [flat(returned[:, i * LEN : (i + 1) * LEN]) for i in range(7)]
    base = 7 * LEN
    sums = returned[:, base + LTXT :].astype(jnp.float32)
    every_modulation = sums[:, :6] + sums[:, 6:]
    table_grad = lax.dot_general(
        every_modulation.reshape(latents, 6 * width),
        picks,
        (((0,), (0,)), ((), ())),
        precision=lax.Precision.HIGHEST,
    ).reshape(6, width, TSTEPS)
    own_branch_grad = own_modulation[:, 5][:, None] * cotangent_all.astype(jnp.float32)

    activated_full, self_mixed_full, cross_mixed_full = unpack(first_full, first_starts)
    expanded_full, qkv_full, probe_grads_full, text_full = unpack(second_full, second_starts)
    shrink_grad = multiply_outer(activated_full, flat(own_branch_grad).astype(low))
    output_grad = multiply_outer(self_mixed_full, features[6])
    merge_grad = multiply_outer(cross_mixed_full, features[5])
    expand_grad, offset_expand = outer_with_sum(features[4], expanded_full)
    qkv_grad, offset_qkv = outer_with_sum(features[2], qkv_full)
    probe_grad, offset_probe = outer_with_sum(features[3], probe_grads_full)
    caption_wide = jnp.pad(caption_all, ((0, 0), (0, LEN - LTXT), (0, 0)))
    text_grad, offset_text = outer_with_sum(flat(caption_wide), text_full)

    def third(values, index):
        return values[..., index * heads_width : (index + 1) * heads_width]

    def token_sum(values):
        return jnp.sum(values.astype(jnp.float32), axis=0)

    return (
        flat(here[:, :LEN]),
        flat(here[:, LEN : 2 * LEN]).astype(jnp.float32),
        flat(here[:, base : base + LTXT]).astype(jnp.float32),
        table_grad,
        jnp.sum(every_modulation, axis=0),
        third(qkv_grad, 0),
        third(qkv_grad, 1),
        third(qkv_grad, 2),
        output_grad,
        probe_grad,
        third(text_grad, 0),
        third(text_grad, 1),
        merge_grad,
        expand_grad,
        shrink_grad,
        third(offset_qkv, 0),
        third(offset_qkv, 2),
        token_sum(features[6]),
        offset_probe,
        third(offset_text, 1),
        token_sum(features[5]),
        offset_expand,
        jnp.sum(flat(own_branch_grad), axis=0),
    )


def solution(mesh):
    return jax.shard_map(
        per_device,
        mesh=mesh,
        in_specs=(
            P("col", "row"),
            P("col", "row"),
            P(),
            P(),
            P(None, "row", None),
            P(None, "row"),
            P("row", "col"),
            P("col"),
            P("row", "col"),
            P("row", "col"),
            P("col"),
            P("col", "row"),
            P("row"),
            P("row", "col"),
            P("col"),
            P("row", "col"),
            P("row", "col"),
            P("col"),
            P("col", "row"),
            P("row"),
            P("row", "col"),
            P("col"),
            P("col", "row"),
            P("row"),
            P("col", "row"),
        ),
        out_specs=(
            P("col", "row"),
            P("col", "row"),
            P("col", "row"),
            P(None, "row", None),
            P(None, "row"),
            P("row", "col"),
            P("row", "col"),
            P("row", "col"),
            P("col", "row"),
            P("row", "col"),
            P("row", "col"),
            P("row", "col"),
            P("col", "row"),
            P("row", "col"),
            P("col", "row"),
            P("col"),
            P("col"),
            P("row"),
            P("col"),
            P("col"),
            P("row"),
            P("col"),
            P("row"),
        ),
        check_vma=False,
    )
```

time: 1880 us -> 535 us (0.28); the launches traced: 1850 us -> 528 us
  waiting for transfers between devices: 1390 us -> 289 us
  blocking collectives: 249 us -> 11.8 us
  matrix products: 132 us -> 92.4 us
  local copies, waits for them, and re-layouts: 38 us -> 72.1 us
  starting transfers between devices: 1.55 us -> 20.9 us
    reduce_scatter x14 -> x0, waiting for transfers between devices: 820 us -> none  [the longest x8 787 us: project(): return lax.psum_scatter(partials, 'row', scatter_dimension=0, tiled=True)]
    all_gather x10 -> x4, waiting for transfers between devices: 467 us -> 156 us  [gather_rows(): return lax.all_gather(values, 'row', axis=0, tiled=True)]
    psum x4 -> x0, blocking collectives: 204 us -> none  [feature_means(): lax.psum((jnp.sum(first_term, axis=1), jnp.sum(second_term, axis=1)), 'row')]
    all_to_all x0 -> x2, waiting for transfers between devices: none -> 113 us  [the longest x1 63.4 us: to_features(): lax.all_to_all(parts.reshape(size * own, rows, -1), 'row', 0, 0, tiled=True)]
    unnamed x28 -> x4, waiting for transfers between devices: 103 us -> 0.07 us
    all_gather x9 -> x1, blocking collectives: 44.8 us -> 11.8 us  [per_device(): lax.all_gather(jnp.concatenate([hidden, cotangent, caption], axis=0), 'co...]
    ppermute x0 -> x7, waiting for transfers between devices: none -> 20.3 us  [col_sum(): other = lax.ppermute(partial.astype(jnp.bfloat16), 'col', [(0, 1), (1, 0)])]
    dot_general x10 -> x7, matrix products: 40.4 us -> 22 us  [multiply(): return jnp.dot(left_side, right_side, preferred_element_type=jnp.float32)]
  transfers between devices with their start and end apart: 26 -> 13, of which waited for: 23 -> 10; matrix products, arithmetic and copies ran while one was open for 8% -> 29% of each run, Pallas kernels for 0% -> 0%
where the time goes in v1:
time: 535 us; the launch traced here: 528 us
  waiting for transfers between devices  289 us (54%)
  matrix products  92.4 us (17%)
  local copies, waits for them, and re-layouts  72.1 us (13%)
  other arithmetic  26.4 us (5%)
  starting transfers between devices  20.9 us (4%)
  between operations  15.3 us (3%)
  blocking collectives  11.8 us (2%)
    all_gather x4, waiting for transfers between devices, gather_rows(): return lax.all_gather(values, 'row', axis=0, tiled=True)  156 us
    all_to_all x1, waiting for transfers between devices, to_features(): lax.all_to_all(parts.reshape(size * own, rows, -1), 'row', 0, 0, tiled=True)  63.4 us
    all_to_all x1, waiting for transfers between devices, to_token_rows(): moved = lax.all_to_all(values, 'row', 0, 0, tiled=True)  50.1 us
    dot_general x7, matrix products, multiply_outer(): lax.dot_general(left_side, right_side, (((0,), (0,)), ((), ())), preferre...  28.3 us
    dot_general x7, matrix products, multiply_back(): lax.dot_general(left_side, right_side, (((1,), (1,)), ((), ())), preferre...  22.9 us
    dot_general x7, matrix products, multiply(): return jnp.dot(left_side, right_side, preferred_element_type=jnp.float32)  22 us
    ppermute x7, waiting for transfers between devices, col_sum(): other = lax.ppermute(partial.astype(jnp.bfloat16), 'col', [(0, 1), (1, 0)])  20.3 us
    unnamed x163, local copies, waits for them, and re-layouts  12.7 us
  transfers between devices with their start and end apart: 13, of which 10 were waited for; matrix products, arithmetic and copies ran while one was open for 29% of the time, Pallas kernels for 0%

profile of v1, /device:TPU:9, one launch (start us, length us, event | category | flops | bytes accessed | tf_op | source)
XLA Modules:
  0.0 528.3 jit_solution(9720706193292686090)
XLA Ops:
  15.5 11.8 %all-gather.1 = bf16[2,3008,72]{1,2,0:T(8,128)(2,1)S(1)} all-gather(bf16[1,3008,72]{1,2,0:T(8,128)(2,1)S(1)} %maximum_bitcast_fusion), channel_id=2, replica_groups=mesh['row'=16,'col'=2] {'col'}, dimensions={0}, use_global_device_ids=true | all-gather | bytes 1299456 | tf_op jit(solution)/shard_map/all_gather | solution.py:221
  32.6 7.5 %all-to-all-start = ((bf16[16,394,72]{1,2,0:T(8,128)(2,1)}), bf16[16,394,72]{1,2,0:T(8,128)(2,1)S(1)}, u32[]{:S(2)}, u32[]{:S(2)}) async-start(bf16[16,394,72]{1,2,0:T(8,128)(2,1)} %copy.156), calls=%async_computation | async-start | bytes 2359296 | tf_op jit(solution)/shard_map/all_to_all | solution.py:143
  41.0 50.1 %all-to-all-done = bf16[16,394,72]{1,2,0:T(8,128)(2,1)S(1)} async-done(((bf16[16,394,72]{1,2,0:T(8,128)(2,1)}), bf16[16,394,72]{1,2,0:T(8,128)(2,1)S(1)}, u32[]{:S(2)}, u32[]{:S(2)}) %all-to-all-start) | async-done | bytes 907808 | tf_op jit(solution)/shard_map/all_to_all | solution.py:143
  94.3 2.7 slice_reduce_fusion.2
  97.0 20.5 %all-gather.7.cloned.1.call-done = bf16[1152,4864]{1,0:T(8,128)(2,1)} async-done(((bf16[72,4864]{1,0:T(8,128)(2,1)}), bf16[1152,4864]{1,0:T(8,128)(2,1)}) %all-gather.7.cloned.1.call-update) | async-done | bytes 11206672 | tf_op jit(solution)/shard_map/all_gather | solution.py:103
  117.5 3.9 fusion.38
  122.2 2.7 fusion.230
  126.0 2.5 fusion.41
  129.0 4.4 collective-permute-done
  136.5 2.9 fusion.232
  142.2 4.9 collective-permute-done.1
  150.2 61.7 %all-gather.9.cloned.1.call-done = bf16[1152,4608]{1,0:T(8,128)(2,1)} async-done(((bf16[72,4608]{1,0:T(8,128)(2,1)}), bf16[1152,4608]{1,0:T(8,128)(2,1)}) %all-gather.9.cloned.1.call-update) | async-done | bytes 10616848 | tf_op jit(solution)/shard_map/all_gather | solution.py:103
  212.0 4.7 multiply_convert_fusion
  218.8 4.5 fusion.78
  227.8 7.2 %collective-permute-done.3 = bf16[128,1152]{1,0:T(8,128)(2,1)S(1)} collective-permute-done((bf16[128,1152]{1,0:T(8,128)(2,1)S(1)}, bf16[128,1152]{1,0:T(8,128)(2,1)S(1)}, u32[]{:S(2)}, u32[]{:S(2)}) %collective-permute-start.3) | collective-permute-done | bytes 294944 | tf_op jit(solution)/shard_map/ppermute | solution.py:108
  243.8 3.0 fusion.234
  277.6 5.4 %fusion.236 = (bf16[128,1152]{1,0:T(8,128)(2,1)}, f32[128,1152]{1,0:T(8,128)}) fusion(bf16[128,2304]{1,0:T(8,128)(2,1)} %copy-done.26, bf16[1152,4608]{1,0:T(8,128)(2,1)} %all-gather.9.cloned.1.call-done), kind=kOutput, calls=%fused_computation.315 | convolution fusion | flops 679624704 | bytes 6782976 | tf_op jit(solution)/shard_map/dot_general | solution.py:21
  285.6 2.9 fusion.237
  289.8 4.3 fusion.235
  294.4 2.8 collective-permute-done.6
  313.8 4.7 concatenate.126
  318.5 6.2 %all-to-all-start.1 = ((bf16[16,1028,72]{1,2,0:T(8,128)(2,1)}), bf16[16,1028,72]{1,2,0:T(8,128)(2,1)S(1)}, u32[]{:S(2)}, u32[]{:S(2)}) async-start(bf16[16,1028,72]{1,2,0:T(8,128)(2,1)} %bitcast.234), calls=%async_computation.1 | async-start | bytes 5308416 | tf_op jit(solution)/shard_map/all_to_all | solution.py:152
  335.9 63.4 %all-to-all-done.1 = bf16[16,1028,72]{1,2,0:T(8,128)(2,1)S(1)} async-done(((bf16[16,1028,72]{1,2,0:T(8,128)(2,1)}), bf16[16,1028,72]{1,2,0:T(8,128)(2,1)S(1)}, u32[]{:S(2)}, u32[]{:S(2)}) %all-to-all-start.1) | async-done | bytes 2368544 | tf_op jit(solution)/shard_map/all_to_all | solution.py:152
  411.0 3.0 fusion.189
  413.9 3.0 fusion.29
  417.0 3.2 fusion.33
  420.2 6.5 %fusion.2 = f32[2304,72]{0,1:T(8,128)} fusion(bf16[2048,3584]{1,0:T(8,128)(2,1)} %all-gather.13.cloned.1.call-done, f32[2048,72]{0,1:T(8,128)S(1)} %bitcast.266, f32[9,8,16,128]{3,2,1,0:T(8,128)S(1)} %bitcast.239), kind=kOutput, calls=%fused_computation.2 | convolution fusion | flops 679772160 | bytes 11280384 | tf_op jit(solution)/shard_map/dot_general | solution.py:27
  426.7 73.3 %all-gather.11.cloned.1.call-done = bf16[2048,5888]{1,0:T(8,128)(2,1)} async-done(((bf16[128,5888]{1,0:T(8,128)(2,1)}), bf16[2048,5888]{1,0:T(8,128)(2,1)}) %all-gather.11.cloned.1.call-update) | async-done | bytes 24117264 | tf_op jit(solution)/shard_map/all_gather | solution.py:103
  500.0 3.3 fusion.8
  504.7 2.3 fusion.31
  508.4 4.5 fusion.6
  514.3 5.5 %fusion.4 = f32[80,2304]{1,0:T(8,128)S(1)} fusion(bf16[2048,5888]{1,0:T(8,128)(2,1)} %all-gather.11.cloned.1.call-done, bf16[2048,72]{0,1:T(8,128)(2,1)S(1)} %bitcast.276), kind=kOutput, calls=%fused_computation.4 | convolution fusion | flops 755302400 | bytes 10469376 | tf_op jit(solution)/shard_map/dot_general | solution.py:27
  (316 shorter events, 123.8 us)
Async XLA Ops:
  7.3 110.2 %all-gather.7.cloned.1.call-start = ((), (), s32[]{:S(2)}) async-start(), calls=%async_computation.2 | async-start | bytes 11907072 | tf_op jit(solution)/shard_map/all_gather | solution.py:103
  30.9 9.2 %copy-start.37 = (bf16[2304,72]{0,1:T(8,128)(2,1)S(1)}, bf16[2304,72]{0,1:T(8,128)(2,1)}, u32[]{:S(2)}) copy-start(bf16[2304,72]{0,1:T(8,128)(2,1)} %param.47) | copy-start | bytes 995332
  30.9 9.2 %copy-start.38 = (bf16[72,2304]{1,0:T(8,128)(2,1)S(1)}, bf16[72,2304]{1,0:T(8,128)(2,1)}, u32[]{:S(2)}) copy-start(bf16[72,2304]{1,0:T(8,128)(2,1)} %param.45) | copy-start | bytes 995332
  32.5 58.8 %copy-start.76 = (s32[16]{0:T(128)S(1)}, s32[16]{0:T(128)}, u32[]{:S(2)}) copy-start(s32[16]{0:T(128)} %param.27) | copy-start | bytes 196
  32.5 59.4 %copy-start.65 = (f32[576]{0:T(1024)S(1)}, f32[576]{0:T(1024)}, u32[]{:S(2)}) copy-start(f32[576]{0:T(1024)} %param.42) | copy-start | bytes 6916
  32.5 59.5 %copy-start.66 = (f32[576]{0:T(1024)S(1)}, f32[576]{0:T(1024)}, u32[]{:S(2)}) copy-start(f32[576]{0:T(1024)} %param.32) | copy-start | bytes 6916
  32.6 59.5 %copy-start.67 = (f32[576]{0:T(1024)S(1)}, f32[576]{0:T(1024)}, u32[]{:S(2)}) copy-start(f32[576]{0:T(1024)} %param.35) | copy-start | bytes 6916
  32.6 58.5 %all-to-all-start = ((bf16[16,394,72]{1,2,0:T(8,128)(2,1)}), bf16[16,394,72]{1,2,0:T(8,128)(2,1)S(1)}, u32[]{:S(2)}, u32[]{:S(2)}) async-start(bf16[16,394,72]{1,2,0:T(8,128)(2,1)} %copy.156), calls=%async_computation | async-start | bytes 2359296 | tf_op jit(solution)/shard_map/all_to_all | solution.py:143
  40.0 171.9 %all-gather.9.cloned.1.call-start = ((), (), s32[]{:S(2)}) async-start(), calls=%async_computation.3 | async-start | bytes 11280384 | tf_op jit(solution)/shard_map/all_gather | solution.py:103
  91.1 322.9 %all-gather.13.cloned.1.call-start = ((), (), s32[]{:S(2)}) async-start(), calls=%async_computation.5 | async-start | bytes 15597568 | tf_op jit(solution)/shard_map/all_gather | solution.py:103
  96.9 24.5 %copy-start.53 = (f32[1152]{0:T(1024)}, f32[1152]{0:T(1024)S(1)}, u32[]{:S(2)}) copy-start(f32[1152]{0:T(1024)S(1)} %get-tuple-element.67) | copy-start | bytes 13828
  97.0 121.9 %copy-start.50 = (f32[1152]{0:T(1024)}, f32[1152]{0:T(1024)S(1)}, u32[]{:S(2)}) copy-start(f32[1152]{0:T(1024)S(1)} %get-tuple-element.61) | copy-start | bytes 13828
  97.0 24.4 %copy-start.60 = (f32[128]{0:T(128)}, f32[128]{0:T(128)S(1)}, u32[]{:S(2)}) copy-start(f32[128]{0:T(128)S(1)} %get-tuple-element.107) | copy-start | bytes 1540
  97.0 24.4 %copy-start.62 = (f32[128]{0:T(128)}, f32[128]{0:T(128)S(1)}, u32[]{:S(2)}) copy-start(f32[128]{0:T(128)S(1)} %get-tuple-element.108) | copy-start | bytes 1540
  124.8 8.5 %collective-permute-start = (bf16[128,1152]{1,0:T(8,128)(2,1)}, bf16[128,1152]{1,0:T(8,128)(2,1)S(1)}, u32[]{:S(2)}, u32[]{:S(2)}) collective-permute-start(bf16[128,1152]{1,0:T(8,128)(2,1)} %get-tuple-element.111), channel_id=1, source_target_pairs={{0,1},{1,0},{2,3},{3,2},{4,5},{5,4},{6,7},{7,6},{8,9},{9,8},{10,11... | collective-permute-start | bytes 884744 | tf_op jit(solution)/shard_map/ppermute | solution.py:108
  139.4 72.6 %copy-start.74 = (f32[2304]{0:T(1024)S(1)}, f32[2304]{0:T(1024)}, u32[]{:S(2)}) copy-start(f32[2304]{0:T(1024)} %param.46) | copy-start | bytes 27652
  139.4 7.7 %collective-permute-start.1 = (bf16[128,1152]{1,0:T(8,128)(2,1)}, bf16[128,1152]{1,0:T(8,128)(2,1)S(1)}, u32[]{:S(2)}, u32[]{:S(2)}) collective-permute-start(bf16[128,1152]{1,0:T(8,128)(2,1)} %get-tuple-element.115), channel_id=1, source_target_pairs={{0,1},{1,0},{2,3},{3,2},{4,5},{5,4},{6,7},{7,6},{8,9},{9,8},{10,11... | collective-permute-start | bytes 884744 | tf_op jit(solution)/shard_map/ppermute | solution.py:108
  218.5 281.4 %all-gather.11.cloned.1.call-start = ((), (), s32[]{:S(2)}) async-start(), calls=%async_computation.4 | async-start | bytes 25624576 | tf_op jit(solution)/shard_map/all_gather | solution.py:103
  226.5 8.5 %collective-permute-start.3 = (bf16[128,1152]{1,0:T(8,128)(2,1)S(1)}, bf16[128,1152]{1,0:T(8,128)(2,1)S(1)}, u32[]{:S(2)}, u32[]{:S(2)}) collective-permute-start(bf16[128,1152]{1,0:T(8,128)(2,1)S(1)} %get-tuple-element.117), channel_id=1, source_target_pairs={{0,1},{1,0},{2,3},{3,2},{4,5},{5,4},{6,7},{7,6},{8,9},{9,8},{10,11... | collective-permute-start | bytes 884744 | tf_op jit(solution)/shard_map/ppermute | solution.py:108
  246.8 10.0 %collective-permute-start.4 = (bf16[128,1152]{1,0:T(8,128)(2,1)}, bf16[128,1152]{1,0:T(8,128)(2,1)}, u32[]{:S(2)}, u32[]{:S(2)}) collective-permute-start(bf16[128,1152]{1,0:T(8,128)(2,1)} %get-tuple-element.119), channel_id=1, source_target_pairs={{0,1},{1,0},{2,3},{3,2},{4,5},{5,4},{6,7},{7,6},{8,9},{9,8},{10,11... | collective-permute-start | bytes 884744 | tf_op jit(solution)/shard_map/ppermute | solution.py:108
  258.9 9.0 %copy-start.28 = (bf16[128,576]{0,1:T(8,128)(2,1)S(1)}, bf16[128,576]{0,1:T(8,128)(2,1)}, u32[]{:S(2)}) copy-start(bf16[128,576]{0,1:T(8,128)(2,1)} %copy-done.27) | copy-start | bytes 442372
  261.2 10.4 %copy-start.18 = (bf16[128,1152]{1,0:T(8,128)(2,1)S(1)}, bf16[128,1152]{1,0:T(8,128)(2,1)}, u32[]{:S(2)}) copy-start(bf16[128,1152]{1,0:T(8,128)(2,1)} %fusion.150) | copy-start | bytes 884740
  261.2 10.4 %copy-start.23 = (bf16[128,576]{1,0:T(8,128)(2,1)S(1)}, bf16[128,576]{1,0:T(8,128)(2,1)}, u32[]{:S(2)}) copy-start(bf16[128,576]{1,0:T(8,128)(2,1)} %copy.184) | copy-start | bytes 442372
  283.0 19.6 %collective-permute-start.2 = (bf16[128,1152]{1,0:T(8,128)(2,1)}, bf16[128,1152]{1,0:T(8,128)(2,1)}, u32[]{:S(2)}, u32[]{:S(2)}) collective-permute-start(bf16[128,1152]{1,0:T(8,128)(2,1)} %get-tuple-element.125), channel_id=1, source_target_pairs={{0,1},{1,0},{2,3},{3,2},{4,5},{5,4},{6,7},{7,6},{8,9},{9,8},{10,11... | collective-permute-start | bytes 884744 | tf_op jit(solution)/shard_map/ppermute | solution.py:108
  288.5 13.1 %copy-start.57 = (f32[1152]{0:T(1024)S(1)}, f32[1152]{0:T(1024)}, u32[]{:S(2)}) copy-start(f32[1152]{0:T(1024)} %get-tuple-element.78) | copy-start | bytes 13828
  288.5 15.7 %copy-start.51 = (f32[1152]{0:T(1024)S(1)}, f32[1152]{0:T(1024)}, u32[]{:S(2)}) copy-start(f32[1152]{0:T(1024)} %copy-done.50) | copy-start | bytes 13828
  288.5 15.7 %copy-start.52 = (f32[1152]{0:T(1024)S(1)}, f32[1152]{0:T(1024)}, u32[]{:S(2)}) copy-start(f32[1152]{0:T(1024)} %get-tuple-element.62) | copy-start | bytes 13828
  288.6 8.7 %collective-permute-start.6 = (bf16[120,1152]{1,0:T(8,128)(2,1)S(1)}, bf16[120,1152]{1,0:T(8,128)(2,1)S(1)}, u32[]{:S(2)}, u32[]{:S(2)}) collective-permute-start(bf16[120,1152]{1,0:T(8,128)(2,1)S(1)} %get-tuple-element.127), channel_id=1, source_target_pairs={{0,1},{1,0},{2,3},{3,2},{4,5},{5,4},{6,7},{7,6},{8,9},{9,8},{10,11... | collective-permute-start | bytes 829448 | tf_op jit(solution)/shard_map/ppermute | solution.py:108
  294.1 9.4 %collective-permute-start.5 = (bf16[128,1152]{1,0:T(8,128)(2,1)}, bf16[128,1152]{1,0:T(8,128)(2,1)S(1)}, u32[]{:S(2)}, u32[]{:S(2)}) collective-permute-start(bf16[128,1152]{1,0:T(8,128)(2,1)} %get-tuple-element.121), channel_id=1, source_target_pairs={{0,1},{1,0},{2,3},{3,2},{4,5},{5,4},{6,7},{7,6},{8,9},{9,8},{10,11... | collective-permute-start | bytes 884744 | tf_op jit(solution)/shard_map/ppermute | solution.py:108
  318.5 80.9 %all-to-all-start.1 = ((bf16[16,1028,72]{1,2,0:T(8,128)(2,1)}), bf16[16,1028,72]{1,2,0:T(8,128)(2,1)S(1)}, u32[]{:S(2)}, u32[]{:S(2)}) async-start(bf16[16,1028,72]{1,2,0:T(8,128)(2,1)} %bitcast.234), calls=%async_computation.1 | async-start | bytes 5308416 | tf_op jit(solution)/shard_map/all_to_all | solution.py:152
  324.7 9.0 %copy-start.4 = (bf16[2,1024,72]{1,2,0:T(8,128)(2,1)S(1)}, bf16[2,1024,72]{1,2,0:T(8,128)(2,1)}, u32[]{:S(2)}) copy-start(bf16[2,1024,72]{1,2,0:T(8,128)(2,1)} %copy-done.3) | copy-start | bytes 884740
  420.2 79.8 %copy-start.42 = (bf16[9,8,16,128]{3,1,2,0:T(8,128)(2,1)S(1)}, bf16[9,8,16,128]{3,1,2,0:T(8,128)(2,1)}, u32[]{:S(2)}) copy-start(bf16[9,8,16,128]{3,1,2,0:T(8,128)(2,1)} %copy.231) | copy-start | bytes 884740
  (58 other events, 275.1 us)
Sparse Core Ops, SparseCore 0:
  13.4 104.0 all-gather.6
  120.3 91.5 all-gather.8
  218.7 111.2 all-gather.12
  331.5 168.4 all-gather.10
